TPU v7x, 256 devices: a whole 4x4x8 slice. The times are simulated.
256 devices in a mesh: dp: 8 (over y, core), expert: 32 (over x, z).
Axes of the slice: x: 4, y: 4, z: 8, core: 2. Of those that a mesh axis runs over, the one named last changes fastest.
Arguments:
- tokens: bfloat16 [2048, 4096], P(('dp', 'expert')), may hold values from -6 to 6
- expert_ids: int32 [2048, 8], P(('dp', 'expert')), may hold values from 0 to 31, all different within a row; in each aligned block of 8 rows (0 to 7, 8 to 15, ...) at most 3 rows name the same one
- gate_values: float32 [2048, 8], P(('dp', 'expert')), may hold values from 0.05 to 1
- w_gate: bfloat16 [32, 4096, 2048], P('expert', None, 'dp'), may hold values from -0.09375 to 0.09375
- w_up: bfloat16 [32, 4096, 2048], P('expert', None, 'dp'), may hold values from -0.09375 to 0.09375
- w_down: bfloat16 [32, 2048, 4096], P('expert', 'dp'), may hold values from -0.125 to 0.125
- s_gate: bfloat16 [4096, 2048], P(None, 'dp'), may hold values from -0.09375 to 0.09375
- s_up: bfloat16 [4096, 2048], P(None, 'dp'), may hold values from -0.09375 to 0.09375
- s_down: bfloat16 [2048, 4096], P('dp'), may hold values from -0.125 to 0.125
Outputs:
- mixed: bfloat16 [2048, 4096], P(('dp', 'expert'))
Inputs may be any that keep to these rules, and one draw needn't show every extreme that they name: `expert_ids`: each row names 8 different experts; the 8 rows of one device name one expert at most 3 times.
All inputs are finite; a program needn't handle non-finite values.
Results may differ from a plain program's by a relative error of at most 0.0054.
Values may be sent and summed in bfloat16 or wider, within the bound.
No kernel may reach another device: no remote copies, remote signals or barrier semaphores. Data moves between devices by JAX's collectives and lax.ppermute only.
A program may use at most 128 MiB of HBM per device.

v0:
```python
import jax
import jax.numpy as jnp
from jax import lax
from jax.sharding import PartitionSpec as P


def swiglu(rows, gate_w, up_w, down_w):
    gate = jnp.dot(rows, gate_w, preferred_element_type=jnp.float32)
    up = jnp.dot(rows, up_w, preferred_element_type=jnp.float32)
    hidden = (jax.nn.silu(gate) * up).astype(jnp.bfloat16)
    return jnp.dot(hidden, down_w, preferred_element_type=jnp.float32)


def slot_tables(route_ids, route_gates, experts, capacity):
    row_count, picks = route_ids.shape
    listed = route_ids.reshape(-1)
    expert_range = jnp.arange(experts, dtype=jnp.int32)
    marks = (listed[:, None] == expert_range[None, :]).astype(jnp.int32)
    earlier = jnp.cumsum(marks, axis=0) - marks
    position = jnp.sum(earlier * marks, axis=1)
    slot_index = (listed * capacity + position).reshape(row_count, picks)
    slot_range = jnp.arange(experts * capacity, dtype=jnp.int32)
    matches = slot_index[:, :, None] == slot_range[None, None, :]
    picker = jnp.any(matches, axis=1).astype(jnp.bfloat16)
    combiner = jnp.sum(jnp.where(matches, route_gates[:, :, None], jnp.float32(0.0)), axis=1)
    return (picker, combiner)


def dispatch_rows(picker, source_rows):
    placed = jnp.einsum("rs,rd->sd", picker, source_rows, preferred_element_type=jnp.float32)
    return placed.astype(jnp.bfloat16)


def per_device(tokens, expert_ids, gate_values, w_gate, w_up, w_down, s_gate, s_up, s_down):
    experts = lax.axis_size("expert")
    groups = lax.axis_size("dp")
    own_rows, width = tokens.shape
    picks = expert_ids.shape[1]
    capacity = max(2, min(own_rows, 3 * own_rows * picks // (2 * experts)))
    gate_local = w_gate[0]
    up_local = w_up[0]
    down_local = w_down[0]
    column = lax.all_gather(tokens, "dp", axis=0, tiled=True)
    column_ids, column_gates = (
        lax.all_gather(expert_ids, "dp", axis=0, tiled=True),
        lax.all_gather(gate_values, "dp", axis=0, tiled=True),
    )
    column_cap = capacity * groups
    picker, combiner = slot_tables(column_ids, column_gates, experts, column_cap)
    outgoing = dispatch_rows(picker, column).reshape(experts, column_cap, width)
    arrived = lax.all_to_all(outgoing, "expert", split_axis=0, concat_axis=0, tiled=True)
    items = arrived.shape[1]
    partial_value = swiglu(
        arrived.reshape(experts * items, width), gate_local, up_local, down_local
    )
    partial_value = partial_value.astype(jnp.bfloat16).reshape(experts, items, width)
    returned = lax.all_to_all(partial_value, "expert", split_axis=0, concat_axis=0, tiled=True)
    returned_rows = returned.reshape(experts * column_cap, width)
    routed = jnp.dot(
        combiner,
        returned_rows.astype(jnp.float32),
        precision=lax.Precision.HIGHEST,
        preferred_element_type=jnp.float32,
    )
    mixed = lax.psum_scatter(
        swiglu(column, s_gate, s_up, s_down) + routed, "dp", scatter_dimension=0, tiled=True
    )
    return mixed.astype(jnp.bfloat16)


def solution(mesh):
    placed = (
        P(("dp", "expert"), None),
        P(("dp", "expert"), None),
        P(("dp", "expert"), None),
        P("expert", None, "dp"),
        P("expert", None, "dp"),
        P("expert", "dp", None),
        P(None, "dp"),
        P(None, "dp"),
        P("dp", None),
    )
    return jax.shard_map(
        per_device, mesh=mesh, in_specs=placed, out_specs=P(("dp", "expert"), None), check_vma=False
    )
```

profile of v0, /device:TPU:2, one launch (start us, length us, event | category | flops | bytes accessed | tf_op | source)
XLA Modules:
  0.0 403.5 jit_solution(12211258155983552361)
XLA Ops:
  6.5 0.0 copy-start
  6.5 13.7 %all_gather.10 = s32[64,8]{1,0:T(8,128)S(1)} all-gather(s32[8,8]{1,0:T(8,128)} %param.10), channel_id=1, replica_groups=mesh['dp'=8,'expert'=32] {'dp'}, dimensions={0}, use_global_device_ids=true | all-gather | bytes 2304 | tf_op jit(solution)/shard_map/all_gather | solution.py:45
  20.2 0.1 eq.42
  20.3 0.1 eq.38
  20.4 1.2 reduce-window.6
  21.6 0.2 slice_reduce_fusion
  21.8 0.1 fusion.24
  22.0 0.1 reduce_sum.21
  22.1 0.5 fusion.5
  22.6 13.3 %all_gather.9 = bf16[64,4096]{1,0:T(8,128)(2,1)S(1)} all-gather(bf16[8,4096]{1,0:T(8,128)(2,1)} %param.9), channel_id=1, replica_groups=mesh['dp'=8,'expert'=32] {'dp'}, dimensions={0}, use_global_device_ids=true | all-gather | bytes 589824 | tf_op jit(solution)/shard_map/all_gather | solution.py:43
  35.9 1.8 convolution_convert_fusion
  37.8 0.0 copy-start.3
  37.8 150.5 %all_to_all.10 = bf16[32,24,4096]{2,1,0:T(8,128)(2,1)S(1)} all-to-all(bf16[32,24,4096]{2,1,0:T(8,128)(2,1)S(1)} %bitcast.49), channel_id=1, replica_groups=mesh['dp'=8,'expert'=32] {'expert'}, dimensions={0} | all-to-all | bytes 12582912 | tf_op jit(solution)/shard_map/all_to_all | solution.py:51
  188.3 0.0 copy-start.1
  188.3 2.7 copy-done.1
  191.0 0.0 copy-done.3
  191.0 2.7 fusion.3
  193.7 0.0 copy-done
  193.7 12.8 %convolution_convert_fusion.1 = bf16[768,4096]{1,0:T(8,128)(2,1)} fusion(bf16[1,256,4096]{2,1,0:T(8,128)(2,1)S(1)} %copy-done, bf16[768,4096]{1,0:T(8,128)(2,1)} %bitcast.52, bf16[1,4096,256]{2,1,0:T(8,128)(2,1)} %param.13, f32[768,256]{1,0:T(8,128)} %fusion.3), kind=kOutput, calls=%fused_computation.1 | convolution fusion | flops 3225550848 | bytes 17563648 | tf_op jit(solution)/shard_map/dot_general | solution.py:11
  206.5 0.0 copy-start.2
  206.5 7.8 %all-to-all-start.1 = ((bf16[32,24,4096]{2,1,0:T(8,128)(2,1)}), bf16[32,24,4096]{2,1,0:T(8,128)(2,1)}, u32[]{:S(2)}, u32[]{:S(2)}) async-start(bf16[32,24,4096]{2,1,0:T(8,128)(2,1)} %bitcast.50), calls=%async_computation.1 | async-start | bytes 12582912 | tf_op jit(solution)/shard_map/all_to_all | solution.py:57
  214.3 0.0 reduce-scatter.2.cloned.1.call-start
  214.4 0.0 copy-done.2
  214.4 13.1 %all_gather.11 = f32[64,8]{1,0:T(8,128)S(1)} all-gather(f32[8,8]{1,0:T(8,128)S(1)} %copy-done.2), channel_id=1, replica_groups=mesh['dp'=8,'expert'=32] {'dp'}, dimensions={0}, use_global_device_ids=true | all-gather | bytes 2304 | tf_op jit(solution)/shard_map/all_gather | solution.py:46
  227.5 0.5 select_reduce_fusion
  228.0 2.1 fusion.34
  230.1 4.7 %fusion.15 = f32[64,4096]{1,0:T(8,128)} fusion(bf16[256,4096]{1,0:T(8,128)(2,1)} %param.17, bf16[64,4096]{1,0:T(8,128)(2,1)S(1)} %all_gather.9, bf16[4096,256]{1,0:T(8,128)(2,1)} %param.16, f32[64,256]{1,0:T(8,128)S(1)} %fusion.34), kind=kOutput, calls=%fused_computation.15 | convolution fusion | flops 268533760 | bytes 5832704 | tf_op jit(solution)/shard_map/dot_general | solution.py:11
  234.7 115.3 %all-to-all-done.1 = bf16[32,24,4096]{2,1,0:T(8,128)(2,1)} async-done(((bf16[32,24,4096]{2,1,0:T(8,128)(2,1)}), bf16[32,24,4096]{2,1,0:T(8,128)(2,1)}, u32[]{:S(2)}, u32[]{:S(2)}) %all-to-all-start.1) | async-done | bytes 6291488 | tf_op jit(solution)/shard_map/all_to_all | solution.py:57
  350.0 7.5 %convolution_add_fusion = f32[64,4096]{1,0:T(8,128)} fusion(f32[64,4096]{1,0:T(8,128)} %fusion.15, f32[64,768]{1,0:T(8,128)S(1)} %select_reduce_fusion, bf16[768,4096]{1,0:T(8,128)(2,1)} %bitcast.7), kind=kOutput, calls=%fused_computation.2 | convolution fusion | flops 2416181248 | bytes 8585216 | tf_op jit(solution)/shard_map/dot_general | solution.py:59
  357.5 0.0 reduce-scatter.2.cloned.1.call-update
  357.6 37.5 %reduce-scatter.2.cloned.1.call-done = f32[8,4096]{1,0:T(8,128)} async-done(((f32[64,4096]{1,0:T(8,128)}), f32[8,4096]{1,0:T(8,128)}) %reduce-scatter.2.cloned.1.call-update) | async-done | bytes 131088 | tf_op jit(solution)/shard_map/reduce_scatter | solution.py:65
  395.1 1.5 convert_element_type.30
  (4 shorter events, 0.1 us)
Async XLA Ops:
  6.5 187.2 %copy-start = (bf16[1,256,4096]{2,1,0:T(8,128)(2,1)S(1)}, bf16[1,256,4096]{2,1,0:T(8,128)(2,1)}, u32[]{:S(2)}) copy-start(bf16[1,256,4096]{2,1,0:T(8,128)(2,1)} %param.14) | copy-start | bytes 6291460
  37.8 153.2 %copy-start.3 = (bf16[1,4096,256]{2,1,0:T(8,128)(2,1)S(1)}, bf16[1,4096,256]{2,1,0:T(8,128)(2,1)}, u32[]{:S(2)}) copy-start(bf16[1,4096,256]{2,1,0:T(8,128)(2,1)} %param.12) | copy-start | bytes 6291460
  188.3 2.7 copy-start.1
  206.5 7.8 %copy-start.2 = (f32[8,8]{1,0:T(8,128)S(1)}, f32[8,8]{1,0:T(8,128)}, u32[]{:S(2)}) copy-start(f32[8,8]{1,0:T(8,128)} %param.11) | copy-start | bytes 772
  206.5 143.5 %all-to-all-start.1 = ((bf16[32,24,4096]{2,1,0:T(8,128)(2,1)}), bf16[32,24,4096]{2,1,0:T(8,128)(2,1)}, u32[]{:S(2)}, u32[]{:S(2)}) async-start(bf16[32,24,4096]{2,1,0:T(8,128)(2,1)} %bitcast.50), calls=%async_computation.1 | async-start | bytes 12582912 | tf_op jit(solution)/shard_map/all_to_all | solution.py:57
  214.3 180.8 %reduce-scatter.2.cloned.1.call-start = ((), (), s32[]{:S(2)}) async-start(), calls=%async_computation.3 | async-start | bytes 1179648 | tf_op jit(solution)/shard_map/reduce_scatter | solution.py:65
Sparse Core Ops, SparseCore 0:
  357.7 37.3 reduce-scatter.1
where the time goes:
time: 404 us; the launch traced here: 403 us
  blocking collectives  191 us (47%)
  waiting for transfers between devices  153 us (38%)
  matrix products  31.6 us (8%)
  between operations  13.5 us (3%)
  starting transfers between devices  7.82 us (2%)
    all_to_all x1, blocking collectives, per_device(): lax.all_to_all(outgoing, 'expert', split_axis=0, concat_axis=0, tiled=True)  151 us
    all_to_all x1, waiting for transfers between devices, per_device(): lax.all_to_all(partial_value, 'expert', split_axis=0, concat_axis=0, tile...  115 us
    reduce_scatter x1, waiting for transfers between devices, per_device(): lax.psum_scatter(swiglu(column, s_gate, s_up, s_down) + routed, 'dp', sca...  37.5 us
    dot_general x2, matrix products, swiglu(): return jnp.dot(hidden, down_w, preferred_element_type=jnp.float32)  17.5 us
    all_gather x1, blocking collectives, per_device(): lax.all_gather(expert_ids, 'dp', axis=0, tiled=True)  13.7 us
    all_gather x1, blocking collectives, per_device(): column = lax.all_gather(tokens, 'dp', axis=0, tiled=True)  13.3 us
    all_gather x1, blocking collectives, per_device(): lax.all_gather(gate_values, 'dp', axis=0, tiled=True)  13.1 us
  transfers between devices with their start and end apart: 2, of which 2 were waited for; matrix products, arithmetic and copies ran while one was open for 2% of the time, Pallas kernels for 0%

commit v1 on v0

--- a/solution.py
+++ b/solution.py
@@ -43,7 +43,9 @@
     column = lax.all_gather(tokens, "dp", axis=0, tiled=True)
     column_ids, column_gates = (
         lax.all_gather(expert_ids, "dp", axis=0, tiled=True),
-        lax.all_gather(gate_values, "dp", axis=0, tiled=True),
+        jnp.concatenate(
+            lax.all_to_all(jnp.stack([gate_values] * lax.axis_size("dp")), "dp", 0, 0), axis=0
+        ),
     )
     column_cap = capacity * groups
     picker, combiner = slot_tables(column_ids, column_gates, experts, column_cap)

time: 404 us -> 411 us (1.017)
  waiting for transfers between devices: 153 us -> 169 us
  blocking collectives: 191 us -> 177 us
    all_to_all x1, waiting for transfers between devices: 115 us -> 134 us  [per_device(): lax.all_to_all(partial_value, 'expert', split_axis=0, concat_axis=0, tile...]
    all_gather x1 -> x0, blocking collectives: 13.1 us -> none  [per_device(): lax.all_gather(gate_values, 'dp', axis=0, tiled=True)]
  transfers between devices with their start and end apart: 2 -> 3, of which waited for: 2 -> 2; matrix products, arithmetic and copies ran while one was open for 2% -> 6% of each run, Pallas kernels for 0% -> 0%
where the time goes in v1:
time: 411 us
  blocking collectives  177 us (43%)
  waiting for transfers between devices  169 us (41%)
  matrix products  33.9 us (8%)
  between operations  13.5 us (3%)
  starting transfers between devices  11.6 us (3%)
    all_to_all x1, blocking collectives, per_device(): lax.all_to_all(outgoing, 'expert', split_axis=0, concat_axis=0, tiled=True)  150 us
    all_to_all x1, waiting for transfers between devices, per_device(): lax.all_to_all(partial_value, 'expert', split_axis=0, concat_axis=0, tile...  134 us
    reduce_scatter x1, waiting for transfers between devices, per_device(): lax.psum_scatter(swiglu(column, s_gate, s_up, s_down) + routed, 'dp', sca...  35.2 us
    dot_general x2, matrix products, swiglu(): return jnp.dot(hidden, down_w, preferred_element_type=jnp.float32)  17.3 us
    all_gather x1, blocking collectives, per_device(): lax.all_gather(expert_ids, 'dp', axis=0, tiled=True)  13.7 us
    all_gather x1, blocking collectives, per_device(): column = lax.all_gather(tokens, 'dp', axis=0, tiled=True)  13.3 us
  transfers between devices with their start and end apart: 3, of which 2 were waited for; matrix products, arithmetic and copies ran while one was open for 6% of the time, Pallas kernels for 0%

profile of v1, /device:TPU:2, one launch (start us, length us, event | category | flops | bytes accessed | tf_op | source)
XLA Modules:
  0.0 410.8 jit_solution(11360459642267480112)
XLA Ops:
  6.5 0.0 copy-start
  6.5 13.7 %all_gather.7 = s32[64,8]{1,0:T(8,128)S(1)} all-gather(s32[8,8]{1,0:T(8,128)} %param.10), channel_id=1, replica_groups=mesh['dp'=8,'expert'=32] {'dp'}, dimensions={0}, use_global_device_ids=true | all-gather | bytes 2304 | tf_op jit(solution)/shard_map/all_gather | solution.py:45
  20.2 0.1 eq.42
  20.3 0.1 eq.38
  20.4 1.2 reduce-window.6
  21.6 0.2 slice_reduce_fusion
  21.8 0.1 fusion.24
  22.0 0.1 reduce_sum.21
  22.1 0.5 fusion.5
  22.6 13.3 %all_gather.6 = bf16[64,4096]{1,0:T(8,128)(2,1)S(1)} all-gather(bf16[8,4096]{1,0:T(8,128)(2,1)} %param.9), channel_id=1, replica_groups=mesh['dp'=8,'expert'=32] {'dp'}, dimensions={0}, use_global_device_ids=true | all-gather | bytes 589824 | tf_op jit(solution)/shard_map/all_gather | solution.py:43
  35.9 1.8 convolution_convert_fusion
  37.8 0.0 copy-start.1
  37.8 150.5 %all_to_all.15 = bf16[32,24,4096]{2,1,0:T(8,128)(2,1)} all-to-all(bf16[32,24,4096]{2,1,0:T(8,128)(2,1)S(1)} %bitcast.50), channel_id=1, replica_groups=mesh['dp'=8,'expert'=32] {'expert'}, dimensions={0} | all-to-all | bytes 12582912 | tf_op jit(solution)/shard_map/all_to_all | solution.py:53
  188.3 0.0 copy-done.1
  188.3 0.6 stack.2
  188.9 3.7 all-to-all-start
  192.6 5.2 %fusion.3 = f32[768,256]{1,0:T(8,128)S(1)} fusion(bf16[768,4096]{1,0:T(8,128)(2,1)} %bitcast.52, bf16[1,4096,256]{2,1,0:T(8,128)(2,1)} %param.12), kind=kOutput, calls=%fused_computation.6 | convolution fusion | flops 1610612736 | bytes 9175040 | tf_op jit(solution)/shard_map/dot_general | solution.py:8
  197.9 0.0 copy-done
  197.9 12.7 %convolution_convert_fusion.1 = bf16[768,4096]{1,0:T(8,128)(2,1)} fusion(bf16[1,256,4096]{2,1,0:T(8,128)(2,1)S(1)} %copy-done, bf16[768,4096]{1,0:T(8,128)(2,1)} %bitcast.53, bf16[1,4096,256]{2,1,0:T(8,128)(2,1)} %param.13, f32[768,256]{1,0:T(8,128)S(1)} %fusion.3), kind=kOutput, calls=%fused_computation.1 | convolution fusion | flops 3225550848 | bytes 17563648 | tf_op jit(solution)/shard_map/dot_general | solution.py:11
  210.5 0.0 all-to-all-done
  210.5 7.6 %all-to-all-start.2 = ((bf16[32,24,4096]{2,1,0:T(8,128)(2,1)}), bf16[32,24,4096]{2,1,0:T(8,128)(2,1)}, u32[]{:S(2)}, u32[]{:S(2)}) async-start(bf16[32,24,4096]{2,1,0:T(8,128)(2,1)} %bitcast.51), calls=%async_computation.2 | async-start | bytes 12582912 | tf_op jit(solution)/shard_map/all_to_all | solution.py:59
  218.2 0.2 reduce-scatter.2.cloned.1.call-start
  218.4 2.1 fusion.34
  220.5 4.7 %fusion.15 = f32[64,4096]{1,0:T(8,128)} fusion(bf16[256,4096]{1,0:T(8,128)(2,1)} %param.17, bf16[64,4096]{1,0:T(8,128)(2,1)S(1)} %all_gather.6, bf16[4096,256]{1,0:T(8,128)(2,1)} %param.16, f32[64,256]{1,0:T(8,128)S(1)} %fusion.34), kind=kOutput, calls=%fused_computation.15 | convolution fusion | flops 268533760 | bytes 5832704 | tf_op jit(solution)/shard_map/dot_general | solution.py:11
  225.1 0.5 select_reduce_fusion
  225.7 134.1 %all-to-all-done.2 = bf16[32,24,4096]{2,1,0:T(8,128)(2,1)} async-done(((bf16[32,24,4096]{2,1,0:T(8,128)(2,1)}), bf16[32,24,4096]{2,1,0:T(8,128)(2,1)}, u32[]{:S(2)}, u32[]{:S(2)}) %all-to-all-start.2) | async-done | bytes 6291488 | tf_op jit(solution)/shard_map/all_to_all | solution.py:59
  359.8 7.5 %convolution_add_fusion = f32[64,4096]{1,0:T(8,128)} fusion(f32[64,4096]{1,0:T(8,128)} %fusion.15, f32[64,768]{1,0:T(8,128)S(1)} %select_reduce_fusion, bf16[768,4096]{1,0:T(8,128)(2,1)} %bitcast.8), kind=kOutput, calls=%fused_computation.2 | convolution fusion | flops 2416181248 | bytes 8585216 | tf_op jit(solution)/shard_map/dot_general | solution.py:61
  367.2 0.0 reduce-scatter.2.cloned.1.call-update
  367.3 35.2 %reduce-scatter.2.cloned.1.call-done = f32[8,4096]{1,0:T(8,128)} async-done(((f32[64,4096]{1,0:T(8,128)}), f32[8,4096]{1,0:T(8,128)}) %reduce-scatter.2.cloned.1.call-update) | async-done | bytes 131088 | tf_op jit(solution)/shard_map/reduce_scatter | solution.py:67
  402.4 1.5 convert_element_type.30
  (4 shorter events, 0.1 us)
Async XLA Ops:
  6.5 191.3 %copy-start = (bf16[1,256,4096]{2,1,0:T(8,128)(2,1)S(1)}, bf16[1,256,4096]{2,1,0:T(8,128)(2,1)}, u32[]{:S(2)}) copy-start(bf16[1,256,4096]{2,1,0:T(8,128)(2,1)} %param.14) | copy-start | bytes 6291460
  37.8 150.5 %copy-start.1 = (f32[8,8]{1,0:T(8,128)S(1)}, f32[8,8]{1,0:T(8,128)}, u32[]{:S(2)}) copy-start(f32[8,8]{1,0:T(8,128)} %param.11) | copy-start | bytes 772
  188.9 21.6 %all-to-all-start = ((f32[8,8,8]{2,1,0:T(8,128)}), f32[8,8,8]{2,1,0:T(8,128)S(1)}, u32[]{:S(2)}, u32[]{:S(2)}) async-start(f32[8,8,8]{2,1,0:T(8,128)} %stack.2), calls=%async_computation | async-start | bytes 65536 | tf_op jit(solution)/shard_map/all_to_all | solution.py:47
  210.5 149.2 %all-to-all-start.2 = ((bf16[32,24,4096]{2,1,0:T(8,128)(2,1)}), bf16[32,24,4096]{2,1,0:T(8,128)(2,1)}, u32[]{:S(2)}, u32[]{:S(2)}) async-start(bf16[32,24,4096]{2,1,0:T(8,128)(2,1)} %bitcast.51), calls=%async_computation.2 | async-start | bytes 12582912 | tf_op jit(solution)/shard_map/all_to_all | solution.py:59
  218.2 184.3 %reduce-scatter.2.cloned.1.call-start = ((), (), s32[]{:S(2)}) async-start(), calls=%async_computation.4 | async-start | bytes 1179648 | tf_op jit(solution)/shard_map/reduce_scatter | solution.py:67
Sparse Core Ops, SparseCore 0:
  367.4 35.0 reduce-scatter.1
